TPU v7x, 32 devices: a whole 2x2x4 slice. The times are simulated.
32 devices in a mesh: vocab: 8 (over y, x, core), hidden: 4 (over z).
Axes of the slice: x: 2, y: 2, z: 4, core: 2. Of those that a mesh axis runs over, the one named last changes fastest.
Arguments:
- token_ids: int32 [4096], P('vocab'), may hold values from 0 to 30719
- table: bfloat16 [30720, 128], P('vocab'), may hold values from -0.25 to 0.25
- projection: bfloat16 [128, 4096], P(None, 'hidden'), may hold values from -0.09375 to 0.09375
- grad_out: bfloat16 [4096, 4096], P('vocab', 'hidden'), may hold values from -6 to 6
Outputs:
- table_grad: float32 [30720, 128], P('vocab', 'hidden')
- projection_grad: float32 [128, 4096], P(None, 'hidden')
All inputs are finite; a program needn't handle non-finite values.
Results may differ from a plain program's by a relative error of at most 0.018.
Values may be sent and summed in bfloat16 or wider, within the bound.
A program may use at most 64 MiB of HBM per device.

v0:
```python
import jax
import jax.numpy as jnp
from jax import lax
from jax.sharding import PartitionSpec as P


def lookup_rows(token_ids, piece):
    count = piece.shape[0]
    inside = (token_ids >= 0) & (token_ids < count)
    picked = jnp.take(piece, jnp.clip(token_ids, 0, count - 1), axis=0)
    return jnp.where(inside[:, None], picked.astype(jnp.float32), 0.0)


def owner_rows(row_count, own_start, carry, pieces):
    grads_piece, ids_piece = pieces
    length = ids_piece.shape[0]
    row_ids = own_start + lax.iota(jnp.int32, row_count)

    def one_block(grads_block, ids_block):
        one_hot = (row_ids[:, None] == ids_block[None, :]).astype(jnp.bfloat16)
        return jnp.dot(one_hot, grads_block, preferred_element_type=jnp.float32)

    block = 2048
    grads_blocks = grads_piece.reshape(length // block, block, grads_piece.shape[1])
    ids_blocks = ids_piece.reshape(length // block, block)

    def scan_step(total, items):
        return (total + one_block(items[0], items[1]), None)

    total, unused = lax.scan(scan_step, carry, (grads_blocks, ids_blocks))
    return total


def on_device(token_ids, table, projection, grad_out):
    partial_grad = jnp.dot(grad_out, projection.T, preferred_element_type=jnp.float32)
    rounded = partial_grad.astype(jnp.bfloat16)
    token_grad = (
        lax.psum_scatter(rounded, "hidden", scatter_dimension=1, tiled=True)
        .astype(jnp.float32)
        .astype(jnp.bfloat16)
    )
    row_count = table.shape[0]
    looked = lookup_rows(token_ids, lax.all_gather(table, "vocab", axis=0, tiled=True))
    embedded = looked.astype(jnp.bfloat16)
    partial_proj = jnp.dot(embedded.T, grad_out, preferred_element_type=jnp.float32)
    projection_grad = lax.psum(partial_proj.astype(jnp.bfloat16), "vocab").astype(jnp.float32)
    own_start = lax.axis_index("vocab") * row_count
    empty = jnp.zeros((row_count, token_grad.shape[1]), jnp.float32)
    table_grad = owner_rows(
        row_count,
        own_start,
        empty,
        (
            lax.all_gather(token_grad, "vocab", axis=0, tiled=True),
            lax.all_gather(token_ids, "vocab", axis=0, tiled=True),
        ),
    )
    return (table_grad, projection_grad)


def solution(mesh):
    placed = (P("vocab"), P("vocab", None), P(None, "hidden"), P("vocab", "hidden"))
    return jax.shard_map(
        on_device,
        mesh=mesh,
        in_specs=placed,
        out_specs=(P("vocab", "hidden"), P(None, "hidden")),
        check_vma=False,
    )
```

profile of v0, /device:TPU:0, one launch (start us, length us, event | category | flops | bytes accessed | tf_op | source)
XLA Modules:
  0.0 138.5 jit_solution(14183271649989522370)
XLA Ops:
  8.0 0.0 copy-start
  8.0 0.0 reduce-scatter.2.cloned.1.call-start
  8.1 1.2 copy-done
  9.2 2.1 %convolution_convert_fusion.1 = bf16[512,128]{0,1:T(8,128)(2,1)} fusion(bf16[512,1024]{1,0:T(8,128)(2,1)S(1)} %copy-done, bf16[128,1024]{1,0:T(8,128)(2,1)} %param.8), kind=kOutput, calls=%fused_computation.13 | convolution fusion | flops 134283264 | bytes 1441792 | tf_op jit(solution)/shard_map/dot_general | solution.py:35
  11.3 0.0 reduce-scatter.2.cloned.1.call-update
  11.3 0.0 all-gather.3.cloned.1.call-start
  11.4 0.5 all-gather.3.cloned.1.call-update
  11.9 0.0 all-reduce.2.cloned.1.call-start
  12.0 10.5 %all-gather = s32[8,1,512]{2,1,0:T(1,128)S(1)} all-gather(s32[1,1,512]{2,1,0:T(1,128)} %bitcast.15), channel_id=1, replica_groups=mesh['vocab'=8,'hidden'=4] {'vocab'}, dimensions={0}, use_global_device_ids=true | all-gather | bytes 18432 | tf_op jit(solution)/shard_map/all_gather | solution.py:55
  22.6 0.7 compare_select_fusion
  23.3 0.7 compare_and_fusion.1
  24.0 9.8 %reduce-scatter.2.cloned.1.call-done = bf16[512,32]{0,1:T(8,128)(2,1)} async-done(((bf16[512,128]{0,1:T(8,128)(2,1)}), bf16[512,32]{0,1:T(8,128)(2,1)}) %reduce-scatter.2.cloned.1.call-update) | async-done | bytes 32784 | tf_op jit(solution)/shard_map/reduce_scatter | solution.py:38
  33.8 9.4 %all_gather.10 = bf16[4096,32]{0,1:T(8,128)(2,1)S(1)} all-gather(bf16[512,32]{0,1:T(8,128)(2,1)} %reduce-scatter.2.cloned.1.call-done), channel_id=1, replica_groups=mesh['vocab'=8,'hidden'=4] {'vocab'}, dimensions={0}, use_global_device_ids=true | all-gather | bytes 294912 | tf_op jit(solution)/shard_map/all_gather | solution.py:54
  43.3 0.5 copy.8
  43.8 25.3 %all-gather.3.cloned.1.call-done = bf16[30720,128]{1,0:T(8,128)(2,1)} async-done(((bf16[3840,128]{1,0:T(8,128)(2,1)}), bf16[30720,128]{1,0:T(8,128)(2,1)}) %all-gather.3.cloned.1.call-update) | async-done | bytes 7864336 | tf_op jit(solution)/shard_map/all_gather | solution.py:43
  69.1 5.3 %gather_fusion = bf16[512,128]{1,0:T(8,128)(2,1)S(1)} fusion(bf16[30720,128]{1,0:T(8,128)(2,1)} %all-gather.3.cloned.1.call-done, s32[1024]{0:T(1024)S(1)} %pad_clamp_fusion), kind=kCustom, calls=%fused_computation | custom fusion | bytes 264192 | tf_op jit(solution)/shard_map/jit(_take)/gather | solution.py:10
  74.4 1.3 convolution_convert_fusion
  75.7 0.0 all-reduce.2.cloned.1.call-update
  75.7 12.5 %while.11 = (s32[]{:T(128)}, f32[3840,32]{0,1:T(8,128)S(1)}, s32[2,2048]{1,0:T(2,128)S(1)}, bf16[2,2048,32]{2,1,0:T(8,128)(2,1)S(1)}, s32[]{:T(128)}, /*index=5*/s32[]{:T(128)}, s32[]{:T(128)}) while((s32[]{:T(128)}, f32[3840,32]{0,1:T(8,128)S(1)}, s32[2,2048]{1,0:T(2,128)S(1)}, bf16[2,2048,32]{2,1,0:T(8,128)(2,1)S(1)}, s32[]{:T(128)}, ...), condition=%wide.region_2.3_spmd.clone, body=%wide.region_1.2_spmd.clone.sunk | while | flops 511430400 | bytes 1563747 | solution.py:30
  75.8 6.2 %fusion.27 = f32[3840,32]{0,1:T(8,128)S(1)} fusion(s32[2048]{0:T(1024)S(1)} %bitcast.14, s32[3840]{0:T(1024)S(1)} %iota_add_fusion.2, bf16[2,2048,32]{2,1,0:T(8,128)(2,1)S(1)} %get-tuple-element.121, s32[]{:T(128)} %get-tuple-element.111, f32[3840,32]{0,1:T(8,128)S(1)} %get-tuple-element.112, pred[]{:T(512)S(6)} %compare.3), kind=kOutput, calls=%fused_computation.6.clone.1 | convolution fusion | flops 511426560 | bytes 1531909 | tf_op jit(solution)/shard_map/while/body/eval_jaxpr/dot_general | solution.py:21
  82.1 6.2 %fusion.27 = f32[3840,32]{0,1:T(8,128)S(1)} fusion(s32[2048]{0:T(1024)S(1)} %bitcast.14, s32[3840]{0:T(1024)S(1)} %iota_add_fusion.2, bf16[2,2048,32]{2,1,0:T(8,128)(2,1)S(1)} %get-tuple-element.121, s32[]{:T(128)} %get-tuple-element.111, f32[3840,32]{0,1:T(8,128)S(1)} %get-tuple-element.112, pred[]{:T(512)S(6)} %compare.3), kind=kOutput, calls=%fused_computation.6.clone.1 | convolution fusion | flops 511426560 | bytes 1531909 | tf_op jit(solution)/shard_map/while/body/eval_jaxpr/dot_general | solution.py:21
  88.3 0.0 copy-start.1
  88.3 41.0 %all-reduce.2.cloned.1.call-done = bf16[128,1024]{1,0:T(8,128)(2,1)} async-done(((bf16[128,1024]{1,0:T(8,128)(2,1)}), bf16[128,1024]{1,0:T(8,128)(2,1)}) %all-reduce.2.cloned.1.call-update) | async-done | bytes 262160 | tf_op jit(solution)/shard_map/psum | solution.py:46
  129.3 1.8 %convert_element_type.22 = f32[128,1024]{1,0:T(8,128)} convert(bf16[128,1024]{1,0:T(8,128)(2,1)} %all-reduce.2.cloned.1.call-done) | non-fusion elementwise | flops 131072 | bytes 786432 | tf_op jit(solution)/shard_map/convert_element_type | solution.py:46
  131.1 0.0 copy-done.1
  (8 shorter events, 0.1 us)
Async XLA Ops:
  8.0 1.2 copy-start
  8.0 25.8 %reduce-scatter.2.cloned.1.call-start = ((), (), s32[]{:S(2)}) async-start(), calls=%async_computation.1 | async-start | bytes 163840 | tf_op jit(solution)/shard_map/reduce_scatter | solution.py:38
  11.3 57.8 %all-gather.3.cloned.1.call-start = ((), (), s32[]{:S(2)}) async-start(), calls=%async_computation.2 | async-start | bytes 8847360 | tf_op jit(solution)/shard_map/all_gather | solution.py:43
  11.9 117.4 %all-reduce.2.cloned.1.call-start = ((), (), s32[]{:S(2)}) async-start(), calls=%async_computation.3 | async-start | bytes 524288 | tf_op jit(solution)/shard_map/psum | solution.py:46
  88.3 42.8 %copy-start.1 = (f32[3840,32]{0,1:T(8,128)}, f32[3840,32]{0,1:T(8,128)S(1)}, u32[]{:S(2)}) copy-start(f32[3840,32]{0,1:T(8,128)S(1)} %get-tuple-element.27) | copy-start | bytes 1474564
Sparse Core Ops, SparseCore 0:
  11.6 22.1 reduce-scatter.1
Sparse Core Ops, SparseCore 1:
  13.7 55.3 all-gather.2
  75.8 53.4 all-reduce.1
where the time goes:
time: 139 us
  waiting for transfers between devices  76.7 us (55%)
  blocking collectives  20 us (14%)
  matrix products  15.8 us (11%)
  between operations  15.5 us (11%)
  local copies, waits for them, and re-layouts  6.99 us (5%)
  other arithmetic  3.25 us (2%)
    psum x1, waiting for transfers between devices, on_device(): lax.psum(partial_proj.astype(jnp.bfloat16), 'vocab').astype(jnp.float32)  41 us
    all_gather x1, waiting for transfers between devices, on_device(): lax.all_gather(table, 'vocab', axis=0, tiled=True)  25.3 us
    dot_general x2, matrix products, one_block(): return jnp.dot(one_hot, grads_block, preferred_element_type=jnp.float32)  12.4 us
    all_gather x1, blocking collectives, on_device(): lax.all_gather(token_ids, 'vocab', axis=0, tiled=True)  10.5 us
    reduce_scatter x1, waiting for transfers between devices, on_device(): lax.psum_scatter(rounded, 'hidden', scatter_dimension=1, tiled=True)  9.83 us
    all_gather x1, blocking collectives, on_device(): lax.all_gather(token_grad, 'vocab', axis=0, tiled=True)  9.44 us
    gather x1, local copies, waits for them, and re-layouts, lookup_rows(): picked = jnp.take(piece, jnp.clip(token_ids, 0, count - 1), axis=0)  5.3 us
  transfers between devices with their start and end apart: 3, of which 3 were waited for; matrix products, arithmetic and copies ran while one was open for 10% of the time, Pallas kernels for 0%

commit v1 on v0

--- a/solution.py
+++ b/solution.py
@@ -43,7 +43,9 @@
     looked = lookup_rows(token_ids, lax.all_gather(table, "vocab", axis=0, tiled=True))
     embedded = looked.astype(jnp.bfloat16)
     partial_proj = jnp.dot(embedded.T, grad_out, preferred_element_type=jnp.float32)
-    projection_grad = lax.psum(partial_proj.astype(jnp.bfloat16), "vocab").astype(jnp.float32)
+    projection_grad = jnp.sum(
+        lax.all_gather(partial_proj.astype(jnp.bfloat16), "vocab"), axis=0
+    ).astype(jnp.float32)
     own_start = lax.axis_index("vocab") * row_count
     empty = jnp.zeros((row_count, token_grad.shape[1]), jnp.float32)
     table_grad = owner_rows(

time: 139 us -> 114 us (0.82)
  waiting for transfers between devices: 76.7 us -> 53.5 us
  blocking collectives: 20 us -> 17.6 us
    psum x1 -> x0, waiting for transfers between devices: 41 us -> none  [on_device(): lax.psum(partial_proj.astype(jnp.bfloat16), 'vocab').astype(jnp.float32)]
    all_gather x1, waiting for transfers between devices: 25.3 us -> 52.7 us  [on_device(): lax.all_gather(table, 'vocab', axis=0, tiled=True)]
    reduce_scatter x1, waiting for transfers between devices: 9.83 us -> 0.03 us  [on_device(): lax.psum_scatter(rounded, 'hidden', scatter_dimension=1, tiled=True)]
    reduce_sum x0 -> x1, other arithmetic: none -> 2.13 us  [on_device(): jnp.sum(lax.all_gather(partial_proj.astype(jnp.bfloat16), 'vocab'), axis=0)]
    all_gather x1, blocking collectives: 10.5 us -> 8.88 us  [on_device(): lax.all_gather(token_ids, 'vocab', axis=0, tiled=True)]
  transfers between devices with their start and end apart: 3 -> 3, of which waited for: 3 -> 1; matrix products, arithmetic and copies ran while one was open for 10% -> 20% of each run, Pallas kernels for 0% -> 0%
where the time goes in v1:
time: 114 us; the launch traced here: 113 us
  waiting for transfers between devices  53.5 us (47%)
  blocking collectives  17.6 us (15%)
  matrix products  15.8 us (14%)
  between operations  15.6 us (14%)
  local copies, waits for them, and re-layouts  6.25 us (5%)
  other arithmetic  4.41 us (4%)
    all_gather x1, waiting for transfers between devices, on_device(): lax.all_gather(table, 'vocab', axis=0, tiled=True)  52.7 us
    dot_general x2, matrix products, one_block(): return jnp.dot(one_hot, grads_block, preferred_element_type=jnp.float32)  12.4 us
    all_gather x1, blocking collectives, on_device(): lax.all_gather(token_ids, 'vocab', axis=0, tiled=True)  8.88 us
    all_gather x1, blocking collectives, on_device(): lax.all_gather(token_grad, 'vocab', axis=0, tiled=True)  8.72 us
    gather x1, local copies, waits for them, and re-layouts, lookup_rows(): picked = jnp.take(piece, jnp.clip(token_ids, 0, count - 1), axis=0)  5.3 us
  transfers between devices with their start and end apart: 3, of which 1 were waited for; matrix products, arithmetic and copies ran while one was open for 20% of the time, Pallas kernels for 0%

profile of v1, /device:TPU:0, one launch (start us, length us, event | category | flops | bytes accessed | tf_op | source)
XLA Modules:
  0.0 113.3 jit_solution(647804122831928286)
XLA Ops:
  8.0 0.0 copy-start
  8.0 0.0 all-gather.5.cloned.1.call-start
  8.1 0.7 all-gather.5.cloned.1.call-update
  8.7 0.0 reduce-scatter.2.cloned.1.call-start
  8.8 0.4 copy-done
  9.2 2.1 %convolution_convert_fusion.1 = bf16[512,128]{0,1:T(8,128)(2,1)} fusion(bf16[512,1024]{1,0:T(8,128)(2,1)S(1)} %copy-done, bf16[128,1024]{1,0:T(8,128)(2,1)} %param.8), kind=kOutput, calls=%fused_computation.13 | convolution fusion | flops 134283264 | bytes 1441792 | tf_op jit(solution)/shard_map/dot_general | solution.py:35
  11.3 0.0 reduce-scatter.2.cloned.1.call-update
  11.3 0.0 all-gather.7.cloned.1.call-start
  11.4 0.7 compare_and_fusion.1
  12.1 0.7 compare_select_fusion
  12.8 52.7 %all-gather.5.cloned.1.call-done = bf16[30720,128]{1,0:T(8,128)(2,1)} async-done(((bf16[3840,128]{1,0:T(8,128)(2,1)}), bf16[30720,128]{1,0:T(8,128)(2,1)}) %all-gather.5.cloned.1.call-update) | async-done | bytes 7864336 | tf_op jit(solution)/shard_map/all_gather | solution.py:43
  65.5 5.3 %gather_fusion = bf16[512,128]{1,0:T(8,128)(2,1)S(1)} fusion(bf16[30720,128]{1,0:T(8,128)(2,1)} %all-gather.5.cloned.1.call-done, s32[1024]{0:T(1024)S(1)} %pad_clamp_fusion), kind=kCustom, calls=%fused_computation | custom fusion | bytes 264192 | tf_op jit(solution)/shard_map/jit(_take)/gather | solution.py:10
  70.8 1.3 %convolution_convert_fusion = bf16[128,1024]{1,0:T(8,128)(2,1)} fusion(bf16[512,1024]{1,0:T(8,128)(2,1)S(1)} %copy-done, bf16[512,128]{1,0:T(8,128)(2,1)S(1)} %gather_fusion, pred[512]{0:T(512)(128)(4,1)S(1)} %get-tuple-element.72, pred[512]{0:T(512)(128)(4,1)S(1)} %get-tuple-element.71), kind=kOutput, calls=%fused_computation.12 | convolution fusion | flops 134610944 | bytes 1442816 | tf_op jit(solution)/shard_map/dot_general | solution.py:45
  72.1 0.0 all-gather.7.cloned.1.call-update
  72.2 8.9 %all-gather.1 = s32[8,1,512]{2,1,0:T(1,128)S(1)} all-gather(s32[1,1,512]{2,1,0:T(1,128)} %bitcast.17), channel_id=1, replica_groups=mesh['vocab'=8,'hidden'=4] {'vocab'}, dimensions={0}, use_global_device_ids=true | all-gather | bytes 18432 | tf_op jit(solution)/shard_map/all_gather | solution.py:57
  81.1 0.0 reduce-scatter.2.cloned.1.call-done
  81.2 8.7 %all_gather.16 = bf16[4096,32]{0,1:T(8,128)(2,1)S(1)} all-gather(bf16[512,32]{0,1:T(8,128)(2,1)} %reduce-scatter.2.cloned.1.call-done), channel_id=1, replica_groups=mesh['vocab'=8,'hidden'=4] {'vocab'}, dimensions={0}, use_global_device_ids=true | all-gather | bytes 294912 | tf_op jit(solution)/shard_map/all_gather | solution.py:56
  89.9 0.5 copy.8
  90.4 12.5 %while.11 = (s32[]{:T(128)}, f32[3840,32]{0,1:T(8,128)S(1)}, s32[2,2048]{1,0:T(2,128)S(1)}, bf16[2,2048,32]{2,1,0:T(8,128)(2,1)S(1)}, s32[]{:T(128)}, /*index=5*/s32[]{:T(128)}, s32[]{:T(128)}) while((s32[]{:T(128)}, f32[3840,32]{0,1:T(8,128)S(1)}, s32[2,2048]{1,0:T(2,128)S(1)}, bf16[2,2048,32]{2,1,0:T(8,128)(2,1)S(1)}, s32[]{:T(128)}, ...), condition=%wide.region_2.3_spmd.clone, body=%wide.region_1.2_spmd.clone.sunk | while | flops 511430400 | bytes 1563747 | solution.py:30
  90.4 6.2 %fusion.27 = f32[3840,32]{0,1:T(8,128)S(1)} fusion(s32[2048]{0:T(1024)S(1)} %bitcast.16, s32[3840]{0:T(1024)S(1)} %iota_add_fusion.2, bf16[2,2048,32]{2,1,0:T(8,128)(2,1)S(1)} %get-tuple-element.121, s32[]{:T(128)} %get-tuple-element.111, f32[3840,32]{0,1:T(8,128)S(1)} %get-tuple-element.112, pred[]{:T(512)S(6)} %compare.3), kind=kOutput, calls=%fused_computation.6.clone.1 | convolution fusion | flops 511426560 | bytes 1531909 | tf_op jit(solution)/shard_map/while/body/eval_jaxpr/dot_general | solution.py:21
  96.7 6.2 %fusion.27 = f32[3840,32]{0,1:T(8,128)S(1)} fusion(s32[2048]{0:T(1024)S(1)} %bitcast.16, s32[3840]{0:T(1024)S(1)} %iota_add_fusion.2, bf16[2,2048,32]{2,1,0:T(8,128)(2,1)S(1)} %get-tuple-element.121, s32[]{:T(128)} %get-tuple-element.111, f32[3840,32]{0,1:T(8,128)S(1)} %get-tuple-element.112, pred[]{:T(512)S(6)} %compare.3), kind=kOutput, calls=%fused_computation.6.clone.1 | convolution fusion | flops 511426560 | bytes 1531909 | tf_op jit(solution)/shard_map/while/body/eval_jaxpr/dot_general | solution.py:21
  102.9 0.0 copy-start.1
  102.9 0.0 all-gather.7.cloned.1.call-done
  102.9 2.1 %reduce_sum.12 = bf16[128,1024]{1,0:T(8,128)(2,1)S(1)} reduce(bf16[8,128,1024]{2,1,0:T(8,128)(2,1)} %bitcast.14, bf16[]{:T(256)} %constant.41.clone.1), dimensions={0}, to_apply=%region_3.4 | reduce | flops 917504 | bytes 2359298 | tf_op jit(solution)/shard_map/reduce_sum | solution.py:46
  105.0 0.8 convert_element_type.24
  105.9 0.0 copy-done.1
  (8 shorter events, 0.1 us)
Async XLA Ops:
  8.0 1.2 %copy-start = (bf16[512,1024]{1,0:T(8,128)(2,1)S(1)}, bf16[512,1024]{1,0:T(8,128)(2,1)}, u32[]{:S(2)}) copy-start(bf16[512,1024]{1,0:T(8,128)(2,1)} %param.9) | copy-start | bytes 3145732
  8.0 57.5 %all-gather.5.cloned.1.call-start = ((), (), s32[]{:S(2)}) async-start(), calls=%async_computation.2 | async-start | bytes 8847360 | tf_op jit(solution)/shard_map/all_gather | solution.py:43
  8.7 72.4 %reduce-scatter.2.cloned.1.call-start = ((), (), s32[]{:S(2)}) async-start(), calls=%async_computation.1 | async-start | bytes 163840 | tf_op jit(solution)/shard_map/reduce_scatter | solution.py:38
  11.3 91.6 %all-gather.7.cloned.1.call-start = ((), (), s32[]{:S(2)}) async-start(), calls=%async_computation.3 | async-start | bytes 2359296 | tf_op jit(solution)/shard_map/all_gather | solution.py:47
  102.9 3.0 %copy-start.1 = (f32[3840,32]{0,1:T(8,128)}, f32[3840,32]{0,1:T(8,128)S(1)}, u32[]{:S(2)}) copy-start(f32[3840,32]{0,1:T(8,128)S(1)} %get-tuple-element.27) | copy-start | bytes 1474564
Sparse Core Ops, SparseCore 0:
  10.7 54.7 all-gather.4
  72.3 28.0 all-gather.6
Sparse Core Ops, SparseCore 1:
  12.0 22.1 reduce-scatter.1
